TPU v7x, 32 devices: a whole 2x2x4 slice. The times are simulated.
32 devices in a mesh: dp: 8 (over y, x, core), mp: 4 (over z).
Axes of the slice: x: 2, y: 2, z: 4, core: 2. Of those that a mesh axis runs over, the one named last changes fastest.
Arguments:
- tokens: bfloat16 [32768, 512], P(('dp', 'mp')), may hold values from -6 to 6
- qkv_weight: bfloat16 [512, 1536], replicated, may hold values from -0.25 to 0.25
- out_weight: bfloat16 [512, 512], replicated, may hold values from -2 to 2
- norm1_gain: float32 [512], replicated, may hold values from 0.1 to 1.9
- norm1_shift: float32 [512], replicated, may hold values from -3 to 3
- norm2_gain: float32 [512], replicated, may hold values from 0.1 to 1.9
- norm2_shift: float32 [512], replicated, may hold values from -3 to 3
- up_weight: bfloat16 [512, 2048], P(None, 'mp'), may hold values from -0.25 to 0.25
- up_bias: bfloat16 [2048], P('mp'), may hold values from -3 to 3
- down_weight: bfloat16 [2048, 512], P('mp'), may hold values from -0.125 to 0.125
- down_bias: float32 [512], replicated, may hold values from -3 to 3
- lengths: int32 [17], replicated, may hold values from 512 to 16384, as said below
- cotangent: bfloat16 [32768, 512], P(('dp', 'mp')), may hold values from -6 to 6
Outputs:
- output: bfloat16 [32768, 512], P(('dp', 'mp'))
- input_grad: bfloat16 [32768, 512], P(('dp', 'mp'))
- qkv_grad: float32 [512, 1536], replicated
- out_grad: float32 [512, 512], replicated
- norm1_gain_grad: float32 [512], replicated
- norm1_shift_grad: float32 [512], replicated
- norm2_gain_grad: float32 [512], replicated
- norm2_shift_grad: float32 [512], replicated
- up_grad: float32 [512, 2048], P(None, 'mp')
- up_bias_grad: float32 [2048], P('mp')
- down_grad: float32 [2048, 512], P('mp')
- down_bias_grad: float32 [512], replicated
Inputs may be any that keep to these rules, and one draw needn't show every extreme that they name: The 17 lengths add up to 32768; 1 of them equal 16384, and the others lie between 512 and 1536, both ends reached.
All inputs are finite; a program needn't handle non-finite values.
Results may differ from a plain program's by a relative error of at most 0.012.
Values may be sent and summed in bfloat16 or wider, within the bound.
No kernel may reach another device: no remote copies, remote signals or barrier semaphores. Data moves between devices by JAX's collectives and lax.ppermute only.
A program may use at most 192 MiB of HBM per device.

v0:
```python
import jax
import jax.numpy as jnp
from jax import lax
from jax.sharding import PartitionSpec as P

HEADS = 8
HEAD_DIM = 64
BLK = 512
NORM_EPS = 1e-05
SCORE_EPS = 1e-06
EXACT_MODE = lax.Precision.HIGHEST


def carried_in(array, axis, combine, identity):
    peers, position = (lax.axis_size(axis), lax.axis_index(axis))
    everything = jax.tree.map(
        lambda part, kind: lax.all_gather(part.astype(kind), axis),
        array,
        (jnp.bfloat16, jnp.bfloat16, jnp.bfloat16),
    )
    start = jax.tree.map(
        lambda part, zero: jnp.broadcast_to(jnp.asarray(zero, part.dtype), part.shape),
        array,
        identity,
    )

    def lap(k, before):
        reached = k < position
        new = combine(
            before, jax.tree.map(lambda part, own: part[k].astype(own.dtype), everything, array)
        )
        return jax.tree.map(lambda a, b: jnp.where(reached, a, b), new, before)

    return lax.fori_loop(0, peers, lap, start)


def carried_in_2(array, axis, join, neutral):
    count = lax.axis_size(axis)
    place = lax.axis_index(axis)
    ahead = count - 1 - place
    gathered = jax.tree.map(
        lambda a, kind: lax.all_gather(a.astype(kind), axis),
        array,
        jax.tree.map(lambda a: jnp.bfloat16 if a.dtype == jnp.float32 else a.dtype, array),
    )
    state = jax.tree.map(lambda a, e: jnp.zeros_like(a) + jnp.asarray(e, a.dtype), array, neutral)

    def one(lap, state):
        source = count - 1 - lap
        return join(
            state,
            jax.tree.map(
                lambda a, own: lax.dynamic_index_in_dim(a, source, 0, False).astype(own.dtype),
                gathered,
                array,
            ),
        )

    return lax.fori_loop(0, ahead, one, state)


def normalize(rows, gain, shift):
    centred = rows - jnp.mean(rows, axis=-1, keepdims=True)
    inv_std = lax.rsqrt(jnp.mean(centred * centred, axis=-1, keepdims=True) + NORM_EPS)
    scaled = centred * inv_std
    return (scaled * gain + shift, scaled, inv_std)


def normalize_back(upstream, scaled, inv_std, gain):
    weighted = upstream * gain
    centred = weighted - jnp.mean(weighted, axis=-1, keepdims=True)
    inner = centred - scaled * jnp.mean(weighted * scaled, axis=-1, keepdims=True)
    return (inner * inv_std, jnp.sum(upstream * scaled, axis=0), jnp.sum(upstream, axis=0))


def feature_map(values):
    return jax.nn.elu(values) + 1.0


def feature_slope(values):
    return jnp.where(values > 0, 1.0, jnp.exp(jnp.minimum(values, 0.0)))


def gelu_slope(values):
    return (
        0.5 * (1.0 + lax.erf(values * 0.7071067811865476))
        + values * jnp.exp(-0.5 * values * values) * 0.3989422804014327
    )


def segment_rows(lengths, first, count):
    ends = jnp.cumsum(lengths)
    starts = ends - lengths
    places = first + jnp.arange(count, dtype=jnp.int32)
    segment = jnp.sum((ends[None, :] <= places[:, None]).astype(jnp.int32), axis=1)
    opening = jnp.sum((starts[None, :] == places[:, None]).astype(jnp.int32), axis=1)
    return (segment, opening)


def block_masks(segment, opening, start):
    block_seg = lax.dynamic_slice_in_dim(segment, start, BLK)
    first_open = lax.dynamic_slice_in_dim(opening, start, 1)[0]
    carried = ((block_seg == block_seg[0]) & (first_open == 0)).astype(jnp.float32)
    ending = (block_seg == block_seg[-1]).astype(jnp.float32)
    places = jnp.arange(BLK)
    allowed = (
        (places[None, :] <= places[:, None]) & (block_seg[None, :] == block_seg[:, None])
    ).astype(jnp.float32)
    return (carried, ending, allowed)


def join_states(earlier, later):
    keep = 1.0 - later[2]
    return (
        later[0] + keep * earlier[0],
        later[1] + keep * earlier[1],
        jnp.maximum(earlier[2], later[2]),
    )


def local(
    tokens,
    qkv_weight,
    out_weight,
    norm1_gain,
    norm1_shift,
    norm2_gain,
    norm2_shift,
    up_weight,
    up_bias,
    down_weight,
    down_bias,
    lengths,
    cotangent,
):
    rows = tokens.shape[0]
    width = tokens.shape[1]
    span = rows * lax.axis_size("mp")
    blocks = span // BLK
    group_first = lax.axis_index("dp") * span
    own_start = lax.axis_index("mp") * rows
    segment, opening = segment_rows(lengths, group_first, span)
    continuing = ((segment == segment[0]) & (opening[0] == 0)).astype(jnp.float32)
    reset = 1.0 - continuing[-1]
    inputs = tokens.astype(jnp.float32)
    normed_one, scaled_one, inv_one = normalize(inputs, norm1_gain, norm1_shift)
    normed_low = normed_one.astype(jnp.bfloat16)
    group_rows = lax.all_gather(normed_low, "mp", axis=0, tiled=True)

    def features(start):
        rows_in = lax.dynamic_slice_in_dim(group_rows, start, BLK)
        projected = jnp.dot(rows_in, qkv_weight, preferred_element_type=jnp.float32)
        query = projected[:, :width].reshape(BLK, HEADS, HEAD_DIM)
        keys = projected[:, width : 2 * width].reshape(BLK, HEADS, HEAD_DIM)
        values = projected[:, 2 * width :].reshape(BLK, HEADS, HEAD_DIM)
        return (query, keys, values)

    def forward_block(carry, index):
        state, total = carry
        start = index * BLK
        query, keys, values = features(start)
        query_low = feature_map(query).astype(jnp.bfloat16)
        key_low = feature_map(keys).astype(jnp.bfloat16)
        value_low = values.astype(jnp.bfloat16)
        carried, ending, allowed = block_masks(segment, opening, start)
        scores = (
            jnp.einsum("ihd,jhd->hij", query_low, key_low, preferred_element_type=jnp.float32)
            * allowed[None]
        )
        query_wide = query_low.astype(jnp.float32)
        numerator = jnp.einsum(
            "hij,jhd->ihd",
            scores.astype(jnp.bfloat16),
            value_low,
            preferred_element_type=jnp.float32,
        )
        numerator = numerator + carried[:, None, None] * jnp.einsum(
            "ihd,hde->ihe", query_wide, state, precision=EXACT_MODE
        )
        denominator = (
            jnp.sum(scores, axis=-1).T
            + carried[:, None] * jnp.einsum("ihd,hd->ih", query_wide, total, precision=EXACT_MODE)
            + SCORE_EPS
        )
        keep = carried[-1]
        key_end = key_low * ending.astype(jnp.bfloat16)[:, None, None]
        new_state = keep * state + jnp.einsum(
            "jhd,jhe->hde", key_end, value_low, preferred_element_type=jnp.float32
        )
        new_total = keep * total + jnp.sum(key_end.astype(jnp.float32), axis=0)
        return ((new_state, new_total), (numerator, denominator, query_low, state, total))

    zero_state = jnp.zeros((HEADS, HEAD_DIM, HEAD_DIM), jnp.float32)
    zero_total = jnp.zeros((HEADS, HEAD_DIM), jnp.float32)
    nothing = jnp.zeros((), jnp.float32)
    (state_end, total_end), kept = lax.scan(
        forward_block, (zero_state, zero_total), jnp.arange(blocks, dtype=jnp.int32)
    )
    numerator = kept[0].reshape(span, HEADS, HEAD_DIM)
    denominator = kept[1].reshape(span, HEADS)
    query_all = kept[2].reshape(span, HEADS, HEAD_DIM)
    block_states = kept[3]
    block_totals = kept[4]
    state_in, total_in, _ = carried_in(
        (state_end, total_end, reset), "dp", join_states, (zero_state, zero_total, nothing)
    )
    query_wide = query_all.astype(jnp.float32)
    numerator = numerator + continuing[:, None, None] * jnp.einsum(
        "ihd,hde->ihe", query_wide, state_in, precision=EXACT_MODE
    )
    denominator = denominator + continuing[:, None] * jnp.einsum(
        "ihd,hd->ih", query_wide, total_in, precision=EXACT_MODE
    )
    context = numerator / denominator[:, :, None]
    context_low = lax.dynamic_slice_in_dim(context.reshape(span, width), own_start, rows).astype(
        jnp.bfloat16
    )
    attended = jnp.dot(context_low, out_weight, preferred_element_type=jnp.float32)
    residual = inputs + attended
    normed_two, scaled_two, inv_two = normalize(residual, norm2_gain, norm2_shift)
    second_low = normed_two.astype(jnp.bfloat16)
    cotangent_wide = cotangent.astype(jnp.float32)
    group_second = lax.all_gather(second_low, "mp", axis=0, tiled=True)
    hidden_in = jnp.dot(group_second, up_weight, preferred_element_type=jnp.float32) + up_bias
    hidden_low = jax.nn.gelu(hidden_in, approximate=False).astype(jnp.bfloat16)
    ffn_out = lax.psum_scatter(
        jnp.dot(hidden_low, down_weight, preferred_element_type=jnp.float32).astype(jnp.bfloat16),
        "mp",
        scatter_dimension=0,
        tiled=True,
    ).astype(jnp.float32)
    group_cotangent = lax.all_gather(cotangent, "mp", axis=0, tiled=True)
    grad_down = jnp.einsum(
        "tf,td->fd", hidden_low, group_cotangent, preferred_element_type=jnp.float32
    )
    grad_hidden = jnp.einsum(
        "td,fd->tf", group_cotangent, down_weight, preferred_element_type=jnp.float32
    )
    hidden_grad = (grad_hidden * gelu_slope(hidden_in)).astype(jnp.bfloat16)
    grad_up_bias = jnp.sum(hidden_grad.astype(jnp.float32), axis=0)
    grad_up = jnp.einsum("td,tf->df", group_second, hidden_grad, preferred_element_type=jnp.float32)
    grad_second = lax.psum_scatter(
        jnp.einsum("tf,df->td", hidden_grad, up_weight, preferred_element_type=jnp.float32).astype(
            jnp.bfloat16
        ),
        "mp",
        scatter_dimension=0,
        tiled=True,
    ).astype(jnp.float32)
    grad_up, grad_up_bias, grad_down = lax.psum((grad_up, grad_up_bias, grad_down), "dp")
    output = (residual + ffn_out + down_bias).astype(jnp.bfloat16)
    grad_second_in, grad_gain_two, grad_shift_two = normalize_back(
        grad_second, scaled_two, inv_two, norm2_gain
    )
    grad_residual = cotangent_wide + grad_second_in
    grad_attended = grad_residual.astype(jnp.bfloat16)
    grad_out = jnp.einsum(
        "ti,to->io", context_low, grad_attended, preferred_element_type=jnp.float32
    )
    grad_context_own = jnp.einsum(
        "to,io->ti", grad_attended, out_weight, preferred_element_type=jnp.float32
    ).astype(jnp.bfloat16)
    grad_context = (
        lax.all_gather(grad_context_own, "mp", axis=0, tiled=True)
        .astype(jnp.float32)
        .reshape(span, HEADS, HEAD_DIM)
    )
    grad_numer = (grad_context / denominator[:, :, None]).astype(jnp.bfloat16)
    grad_denom = -jnp.sum(grad_context * context, axis=-1) / denominator
    local_state = jnp.einsum(
        "ihd,ihe->hde",
        query_all * continuing.astype(jnp.bfloat16)[:, None, None],
        grad_numer,
        preferred_element_type=jnp.float32,
    )
    local_total = jnp.einsum(
        "ih,ihd->hd", continuing[:, None] * grad_denom, query_wide, precision=EXACT_MODE
    )
    state_back, total_back, _ = carried_in_2(
        (local_state, local_total, reset), "dp", join_states, (zero_state, zero_total, nothing)
    )
    prior = jnp.concatenate([jnp.ones((1,), jnp.float32), continuing[BLK - 1 :: BLK][:-1]])
    true_states = block_states + prior[:, None, None, None] * state_in[None]
    true_totals = block_totals + prior[:, None, None] * total_in[None]

    def back_block(carry, index):
        state_grad, total_grad = carry
        start = index * BLK
        query, keys, values = features(start)
        query_low = feature_map(query).astype(jnp.bfloat16)
        key_low = feature_map(keys).astype(jnp.bfloat16)
        value_low = values.astype(jnp.bfloat16)
        carried, ending, allowed = block_masks(segment, opening, start)
        state = true_states[index]
        total = true_totals[index]
        numer_grad = lax.dynamic_slice_in_dim(grad_numer, start, BLK)
        denom_grad = lax.dynamic_slice_in_dim(grad_denom, start, BLK)
        scores = (
            jnp.einsum("ihd,jhd->hij", query_low, key_low, preferred_element_type=jnp.float32)
            * allowed[None]
        )
        weights = scores.astype(jnp.bfloat16)
        weight_grad = (
            jnp.einsum("ihe,jhe->hij", numer_grad, value_low, preferred_element_type=jnp.float32)
            + denom_grad.T[:, :, None]
        )
        score_grad = weight_grad.astype(jnp.bfloat16) * allowed.astype(jnp.bfloat16)[None]
        query_wide_blk = query_low.astype(jnp.float32)
        numer_wide = numer_grad.astype(jnp.float32)
        query_grad = jnp.einsum(
            "hij,jhd->ihd", score_grad, key_low, preferred_element_type=jnp.float32
        )
        query_grad = query_grad + carried[:, None, None] * (
            jnp.einsum("ihe,hde->ihd", numer_wide, state, precision=EXACT_MODE)
            + denom_grad[:, :, None] * total[None]
        )
        key_grad = jnp.einsum(
            "hij,ihd->jhd", score_grad, query_low, preferred_element_type=jnp.float32
        )
        key_grad = key_grad + ending[:, None, None] * (
            jnp.einsum(
                "jhe,hde->jhd", value_low.astype(jnp.float32), state_grad, precision=EXACT_MODE
            )
            + total_grad[None]
        )
        value_grad = jnp.einsum(
            "hij,ihd->jhd", weights, numer_grad, preferred_element_type=jnp.float32
        )
        value_grad = value_grad + ending[:, None, None] * jnp.einsum(
            "jhd,hde->jhe", key_low.astype(jnp.float32), state_grad, precision=EXACT_MODE
        )
        keep = carried[-1]
        prev_state = keep * state_grad + jnp.einsum(
            "ihd,ihe->hde",
            query_low * carried.astype(jnp.bfloat16)[:, None, None],
            numer_grad,
            preferred_element_type=jnp.float32,
        )
        prev_total = keep * total_grad + jnp.einsum(
            "ih,ihd->hd", carried[:, None] * denom_grad, query_wide_blk, precision=EXACT_MODE
        )
        joined = jnp.concatenate(
            [
                (query_grad * feature_slope(query)).reshape(BLK, width),
                (key_grad * feature_slope(keys)).reshape(BLK, width),
                value_grad.reshape(BLK, width),
            ],
            axis=1,
        )
        return ((prev_state, prev_total), joined.astype(jnp.bfloat16))

    _, grad_blocks = lax.scan(
        back_block, (state_back, total_back), jnp.arange(blocks, dtype=jnp.int32), reverse=True
    )
    grad_projected = lax.dynamic_slice_in_dim(grad_blocks.reshape(span, 3 * width), own_start, rows)
    grad_qkv = jnp.einsum(
        "td,tk->dk", normed_low, grad_projected, preferred_element_type=jnp.float32
    )
    grad_first = jnp.einsum(
        "tk,dk->td", grad_projected, qkv_weight, preferred_element_type=jnp.float32
    )
    grad_first_in, grad_gain_one, grad_shift_one = normalize_back(
        grad_first, scaled_one, inv_one, norm1_gain
    )
    input_grad = (grad_residual + grad_first_in).astype(jnp.bfloat16)
    grad_down_bias = jnp.sum(cotangent_wide, axis=0)
    summed = lax.psum(
        (
            grad_qkv,
            grad_out,
            grad_gain_one,
            grad_shift_one,
            grad_gain_two,
            grad_shift_two,
            grad_down_bias,
        ),
        ("dp", "mp"),
    )
    return (
        output,
        input_grad,
        summed[0],
        summed[1],
        summed[2],
        summed[3],
        summed[4],
        summed[5],
        grad_up,
        grad_up_bias,
        grad_down,
        summed[6],
    )


def solution(mesh):
    in_specs = (
        P(("dp", "mp"), None),
        P(),
        P(),
        P(),
        P(),
        P(),
        P(),
        P(None, "mp"),
        P("mp"),
        P("mp", None),
        P(),
        P(),
        P(("dp", "mp"), None),
    )
    out_specs = (
        P(("dp", "mp"), None),
        P(("dp", "mp"), None),
        P(),
        P(),
        P(),
        P(),
        P(),
        P(),
        P(None, "mp"),
        P("mp"),
        P("mp", None),
        P(),
    )
    return jax.shard_map(local, mesh=mesh, in_specs=in_specs, out_specs=out_specs, check_vma=False)
```

profile of v0, /device:TPU:0, one launch (start us, length us, event | category | flops | bytes accessed | tf_op | source)
XLA Modules:
  0.0 1671.2 jit_solution(14207868749321259398)
XLA Ops:
  17.8 15.2 all-reduce
  33.1 62.3 %all-gather.9.cloned.1.call-done = bf16[4096,512]{0,1:T(8,128)(2,1)} async-done(((bf16[1024,512]{0,1:T(8,128)(2,1)}), bf16[4096,512]{0,1:T(8,128)(2,1)}) %all-gather.9.cloned.1.call-update) | async-done | bytes 4194320 | tf_op jit(solution)/shard_map/all_gather | solution.py:148
  101.9 482.7 %while.75 = (s32[]{:T(128)}, f32[8,64,64]{2,1,0:T(8,128)S(1)}, f32[8,64]{1,0:T(8,128)S(1)}, f32[8,512,8,64]{1,0,3,2:T(8,128)}, f32[8,512,8]{1,2,0:T(8,128)}, /*i...) while((s32[]{:T(128)}, f32[8,64,64]{2,1,0:T(8,128)S(1)}, ...), condition=%wide.region_8.9_spmd.clone, body=%wide.region_5.8_spmd.clone.sunk | while | flops 1599254528 | bytes 64349520 | solution.py:196
  133.0 21.8 %dynamic_update_slice.51 = f32[8,512,8,64]{1,0,3,2:T(8,128)} dynamic-update-slice(f32[8,512,8,64]{1,0,3,2:T(8,128)} %get-tuple-element.1293, f32[1,512,8,64]{1,0,3,2:T(1,128)S(1)} %copy.224, s32[]{:T(128)} %get-tuple-element.1290, s32[]{:T(128)} %constant.253.clone.1..sunk.2, s32[]{:T(128)} %constant.253.clone.1..sunk.2, s32[]{:T(128)} %constant.253.clone.1..sunk.2) | dynamic-update-slice | bytes 2097156 | tf_op jit(solution)/shard_map/while/body/jit(dynamic_update_index_in_dim)/dynamic_update_slice | solution.py:196
  193.4 21.8 %dynamic_update_slice.51 = f32[8,512,8,64]{1,0,3,2:T(8,128)} dynamic-update-slice(f32[8,512,8,64]{1,0,3,2:T(8,128)} %get-tuple-element.1293, f32[1,512,8,64]{1,0,3,2:T(1,128)S(1)} %copy.224, s32[]{:T(128)} %get-tuple-element.1290, s32[]{:T(128)} %constant.253.clone.1..sunk.2, s32[]{:T(128)} %constant.253.clone.1..sunk.2, s32[]{:T(128)} %constant.253.clone.1..sunk.2) | dynamic-update-slice | bytes 2097156 | tf_op jit(solution)/shard_map/while/body/jit(dynamic_update_index_in_dim)/dynamic_update_slice | solution.py:196
  253.7 21.8 %dynamic_update_slice.51 = f32[8,512,8,64]{1,0,3,2:T(8,128)} dynamic-update-slice(f32[8,512,8,64]{1,0,3,2:T(8,128)} %get-tuple-element.1293, f32[1,512,8,64]{1,0,3,2:T(1,128)S(1)} %copy.224, s32[]{:T(128)} %get-tuple-element.1290, s32[]{:T(128)} %constant.253.clone.1..sunk.2, s32[]{:T(128)} %constant.253.clone.1..sunk.2, s32[]{:T(128)} %constant.253.clone.1..sunk.2) | dynamic-update-slice | bytes 2097156 | tf_op jit(solution)/shard_map/while/body/jit(dynamic_update_index_in_dim)/dynamic_update_slice | solution.py:196
  314.0 21.8 %dynamic_update_slice.51 = f32[8,512,8,64]{1,0,3,2:T(8,128)} dynamic-update-slice(f32[8,512,8,64]{1,0,3,2:T(8,128)} %get-tuple-element.1293, f32[1,512,8,64]{1,0,3,2:T(1,128)S(1)} %copy.224, s32[]{:T(128)} %get-tuple-element.1290, s32[]{:T(128)} %constant.253.clone.1..sunk.2, s32[]{:T(128)} %constant.253.clone.1..sunk.2, s32[]{:T(128)} %constant.253.clone.1..sunk.2) | dynamic-update-slice | bytes 2097156 | tf_op jit(solution)/shard_map/while/body/jit(dynamic_update_index_in_dim)/dynamic_update_slice | solution.py:196
  374.4 21.8 %dynamic_update_slice.51 = f32[8,512,8,64]{1,0,3,2:T(8,128)} dynamic-update-slice(f32[8,512,8,64]{1,0,3,2:T(8,128)} %get-tuple-element.1293, f32[1,512,8,64]{1,0,3,2:T(1,128)S(1)} %copy.224, s32[]{:T(128)} %get-tuple-element.1290, s32[]{:T(128)} %constant.253.clone.1..sunk.2, s32[]{:T(128)} %constant.253.clone.1..sunk.2, s32[]{:T(128)} %constant.253.clone.1..sunk.2) | dynamic-update-slice | bytes 2097156 | tf_op jit(solution)/shard_map/while/body/jit(dynamic_update_index_in_dim)/dynamic_update_slice | solution.py:196
  434.7 21.8 %dynamic_update_slice.51 = f32[8,512,8,64]{1,0,3,2:T(8,128)} dynamic-update-slice(f32[8,512,8,64]{1,0,3,2:T(8,128)} %get-tuple-element.1293, f32[1,512,8,64]{1,0,3,2:T(1,128)S(1)} %copy.224, s32[]{:T(128)} %get-tuple-element.1290, s32[]{:T(128)} %constant.253.clone.1..sunk.2, s32[]{:T(128)} %constant.253.clone.1..sunk.2, s32[]{:T(128)} %constant.253.clone.1..sunk.2) | dynamic-update-slice | bytes 2097156 | tf_op jit(solution)/shard_map/while/body/jit(dynamic_update_index_in_dim)/dynamic_update_slice | solution.py:196
  495.0 21.8 %dynamic_update_slice.51 = f32[8,512,8,64]{1,0,3,2:T(8,128)} dynamic-update-slice(f32[8,512,8,64]{1,0,3,2:T(8,128)} %get-tuple-element.1293, f32[1,512,8,64]{1,0,3,2:T(1,128)S(1)} %copy.224, s32[]{:T(128)} %get-tuple-element.1290, s32[]{:T(128)} %constant.253.clone.1..sunk.2, s32[]{:T(128)} %constant.253.clone.1..sunk.2, s32[]{:T(128)} %constant.253.clone.1..sunk.2) | dynamic-update-slice | bytes 2097156 | tf_op jit(solution)/shard_map/while/body/jit(dynamic_update_index_in_dim)/dynamic_update_slice | solution.py:196
  555.3 21.8 %dynamic_update_slice.51 = f32[8,512,8,64]{1,0,3,2:T(8,128)} dynamic-update-slice(f32[8,512,8,64]{1,0,3,2:T(8,128)} %get-tuple-element.1293, f32[1,512,8,64]{1,0,3,2:T(1,128)S(1)} %copy.224, s32[]{:T(128)} %get-tuple-element.1290, s32[]{:T(128)} %constant.253.clone.1..sunk.2, s32[]{:T(128)} %constant.253.clone.1..sunk.2, s32[]{:T(128)} %constant.253.clone.1..sunk.2) | dynamic-update-slice | bytes 2097156 | tf_op jit(solution)/shard_map/while/body/jit(dynamic_update_index_in_dim)/dynamic_update_slice | solution.py:196
  584.6 10.9 all-gather
  595.5 9.1 all-gather.1
  604.6 22.9 %while.76 = (s32[]{:T(128)}, f32[8,64,64]{2,1,0:T(8,128)}, f32[8,64]{1,0:T(8,128)S(1)}, s32[]{:T(128)}, bf16[8,8,64,64]{3,2,1,0:T(8,128)(2,1)S(1)}, /*index=5*/b...) while((s32[]{:T(128)}, f32[8,64,64]{2,1,0:T(8,128)}, ...), condition=%wide.region_10.11_spmd.clone, body=%wide.region_9.10_spmd.clone.sunk | while | flops 166405 | bytes 332957 | solution.py:34
  632.4 9.4 reshape.432
  660.8 76.4 %all-gather.11.cloned.1.call-done = bf16[4096,512]{0,1:T(8,128)(2,1)} async-done(((bf16[1024,512]{0,1:T(8,128)(2,1)}), bf16[4096,512]{0,1:T(8,128)(2,1)}) %all-gather.11.cloned.1.call-update) | async-done | bytes 4194320 | tf_op jit(solution)/shard_map/all_gather | solution.py:223
  737.2 22.8 %fusion.89 = (bf16[4096,512]{1,0:T(8,128)(2,1)}, f32[4096,512]{1,0:T(8,128)}) fusion(f32[512]{0:T(512)} %convert_element_type.335, bf16[4096,512]{0,1:T(8,128)(2,1)} %all-gather.11.cloned.1.call-done, bf16[512,512]{1,0:T(8,128)(2,1)S(1)} %copy-done), kind=kOutput, calls=%fused_computation.135 | convolution fusion | flops 2285895680 | bytes 17303552 | tf_op jit(solution)/shard_map/dot_general | solution.py:224
  760.0 58.0 %all-gather.13.cloned.1.call-done = bf16[4096,512]{1,0:T(8,128)(2,1)} async-done(((bf16[1024,512]{1,0:T(8,128)(2,1)}), bf16[4096,512]{1,0:T(8,128)(2,1)}) %all-gather.13.cloned.1.call-update) | async-done | bytes 4194320 | tf_op jit(solution)/shard_map/all_gather | solution.py:232
  818.1 8.9 convert_reduce_fusion.1
  840.9 10.4 all-gather.15.cloned.1.call-start
  853.7 55.1 %reduce-scatter.5.cloned.1.call-done = bf16[1024,512]{0,1:T(8,128)(2,1)} async-done(((bf16[4096,512]{0,1:T(8,128)(2,1)}), bf16[1024,512]{0,1:T(8,128)(2,1)}) %reduce-scatter.5.cloned.1.call-update) | async-done | bytes 1048592 | tf_op jit(solution)/shard_map/reduce_scatter | solution.py:242
  911.5 76.8 %reduce-scatter.3.cloned.1.call-done = bf16[1024,512]{0,1:T(8,128)(2,1)} async-done(((bf16[4096,512]{0,1:T(8,128)(2,1)}), bf16[1024,512]{0,1:T(8,128)(2,1)}) %reduce-scatter.3.cloned.1.call-update) | async-done | bytes 1048592 | tf_op jit(solution)/shard_map/reduce_scatter | solution.py:226
  1011.1 66.3 %all-gather.15.cloned.1.call-done = bf16[4096,512]{1,0:T(8,128)(2,1)} async-done(((bf16[1024,512]{1,0:T(8,128)(2,1)}), bf16[4096,512]{1,0:T(8,128)(2,1)}) %all-gather.15.cloned.1.call-update) | async-done | bytes 4194320 | tf_op jit(solution)/shard_map/all_gather | solution.py:264
  1077.4 7.1 copy.158
  1084.4 7.8 multiply_reduce_fusion.1
  1098.1 8.9 all-gather.3
  1111.1 13.4 all-gather.2
  1124.5 9.7 while.73
  1139.8 371.0 %while.74 = (s32[]{:T(128)}, f32[8,64,64]{2,1,0:T(8,128)S(1)}, f32[8,64]{1,0:T(8,128)S(1)}, bf16[8,512,1536]{2,1,0:T(8,128)(2,1)}, s32[8]{0:T(128)S(1)}, /*index...) while((s32[]{:T(128)}, f32[8,64,64]{2,1,0:T(8,128)S(1)}, ...), condition=%wide.region_21.22_spmd, body=%wide.region_20.21_spmd.sunk | while | flops 2815500288 | bytes 89005016 | solution.py:352
  1517.2 12.9 psum.77
  1546.3 38.9 %all-reduce.1 = (f32[512]{0:T(512)}, f32[512]{0:T(512)}, f32[512]{0:T(512)}, f32[512]{0:T(512)}, f32[512]{0:T(512)}) all-reduce(f32[512]{0:T(512)S(1)} %get-tuple-element.848, f32[512]{0:T(512)S(1)} %get-tuple-element.977, f32[512]{0:T(512)S(1)} %copy-done.48, f32[512]{0:T(512)S(1)} %copy-done.49, ...), channel_id=1, replica_groups=mesh['dp'=8,'mp'=4] {'dp','mp'}, use_global_device_ids=true, to_apply=%region_27.28 | all-reduce | flops 2560 | bytes 20480 | tf_op jit(solution)/shard_map/psum | solution.py:367
  1585.2 71.9 %all-reduce.7.cloned.1.call-done = (f32[512,1536]{1,0:T(8,128)}, f32[512,512]{1,0:T(8,128)}) async-done(((f32[512,1536]{1,0:T(8,128)}, f32[512,512]{1,0:T(8,128)}), (f32[512,1536]{1,0:T(8,128)}, f32[512,512]{1,0:T(8,128)})) %all-reduce.7.cloned.1.call-update) | async-done | bytes 4194320 | tf_op jit(solution)/shard_map/psum | solution.py:367
  (757 shorter events, 789.9 us)
Async XLA Ops:
  7.2 730.0 %copy-start = (bf16[512,512]{1,0:T(8,128)(2,1)S(1)}, bf16[512,512]{1,0:T(8,128)(2,1)}, u32[]{:S(2)}) copy-start(bf16[512,512]{1,0:T(8,128)(2,1)} %param.28) | copy-start | bytes 1572868
  7.2 8.6 copy-start.59
  7.2 88.1 %all-gather.9.cloned.1.call-start = ((), (), s32[]{:S(2)}) async-start(), calls=%async_computation.2 | async-start | bytes 5242880 | tf_op jit(solution)/shard_map/all_gather | solution.py:148
  8.8 93.1 %copy-start.7 = (bf16[1024,512]{0,1:T(8,128)(2,1)}, bf16[1024,512]{0,1:T(8,128)(2,1)S(1)}, u32[]{:S(2)}) copy-start(bf16[1024,512]{0,1:T(8,128)(2,1)S(1)} %copy.149) | copy-start | bytes 3145732
  11.8 725.5 %all-gather.11.cloned.1.call-start = ((), (), s32[]{:S(2)}) async-start(), calls=%async_computation.3 | async-start | bytes 5242880 | tf_op jit(solution)/shard_map/all_gather | solution.py:223
  15.2 86.6 %copy-start.28 = (f32[4096]{0:T(1024)}, f32[4096]{0:T(1024)S(1)}, u32[]{:S(2)}) copy-start(f32[4096]{0:T(1024)S(1)} %get-tuple-element.953) | copy-start | bytes 49156
  584.6 11.0 copy-start.45
  627.6 14.3 copy-start.26
  632.4 13.5 copy-start.29
  632.4 13.5 copy-start.31
  646.0 7.0 copy-start.8
  646.1 7.0 copy-start.22
  658.8 159.3 %all-gather.13.cloned.1.call-start = ((), (), s32[]{:S(2)}) async-start(), calls=%async_computation.5 | async-start | bytes 5242880 | tf_op jit(solution)/shard_map/all_gather | solution.py:232
  659.5 249.3 %reduce-scatter.5.cloned.1.call-start = ((), (), s32[]{:S(2)}) async-start(), calls=%async_computation.6 | async-start | bytes 5242880 | tf_op jit(solution)/shard_map/reduce_scatter | solution.py:242
  833.3 154.9 %reduce-scatter.3.cloned.1.call-start = ((), (), s32[]{:S(2)}) async-start(), calls=%async_computation.4 | async-start | bytes 5242880 | tf_op jit(solution)/shard_map/reduce_scatter | solution.py:226
  840.9 67.9 %copy-start.33 = (f32[1024]{0:T(1024)S(1)}, f32[1024]{0:T(1024)}, u32[]{:S(2)}) copy-start(f32[1024]{0:T(1024)} %copy-done.32) | copy-start | bytes 12292
  840.9 67.9 %copy-start.37 = (f32[1024]{0:T(1024)S(1)}, f32[1024]{0:T(1024)}, u32[]{:S(2)}) copy-start(f32[1024]{0:T(1024)} %copy-done.36) | copy-start | bytes 12292
  840.9 67.9 %copy-start.42 = (f32[512]{0:T(512)S(1)}, f32[512]{0:T(512)}, u32[]{:S(2)}) copy-start(f32[512]{0:T(512)} %param.26) | copy-start | bytes 6148
  840.9 147.3 %copy-start.51 = (f32[512]{0:T(512)S(1)}, f32[512]{0:T(512)}, u32[]{:S(2)}) copy-start(f32[512]{0:T(512)} %param.31) | copy-start | bytes 6148
  840.9 236.4 %all-gather.15.cloned.1.call-start = ((), (), s32[]{:S(2)}) async-start(), calls=%async_computation.7 | async-start | bytes 5242880 | tf_op jit(solution)/shard_map/all_gather | solution.py:264
  996.0 589.2 %all-reduce.9.cloned.1.call-start = ((), (), s32[]{:S(2)}) async-start(), calls=%async_computation.9 | async-start | bytes 4194304 | tf_op jit(solution)/shard_map/psum | solution.py:250
  1007.7 649.3 %all-reduce.7.cloned.1.call-start = ((), (), s32[]{:S(2)}) async-start(), calls=%async_computation.8 | async-start | bytes 8388608 | tf_op jit(solution)/shard_map/psum | solution.py:367
  1084.4 22.6 %copy-start.5 = (f32[4096,512]{0,1:T(8,128)S(1)}, f32[4096,512]{0,1:T(8,128)}, u32[]{:S(2)}) copy-start(f32[4096,512]{0,1:T(8,128)} %copy.158) | copy-start | bytes 25165828
  1109.8 14.7 copy-start.58
  1150.4 5.8 copy-start.4
  1335.7 5.8 copy-start.4
  1382.1 5.8 copy-start.4
  1428.5 5.8 copy-start.4
  1474.8 5.8 copy-start.4
  1516.5 13.6 copy-start.20
  1657.0 5.9 copy-start.23
  1657.1 6.8 copy-start.1
  (65 other events, 193.6 us)
Sparse Core Ops, SparseCore 0:
  11.9 83.4 all-gather.8
  658.9 78.2 all-gather.10
  738.8 79.2 all-gather.12
  833.4 75.2 reduce-scatter.4
  910.9 77.2 reduce-scatter.2
  996.1 81.2 all-gather.14
  1080.7 61.3 all-reduce.8
  1516.7 140.3 all-reduce.6
where the time goes:
time: 1690 us; the launch traced here: 1670 us
  waiting for transfers between devices  468 us (28%)
  local copies, waits for them, and re-layouts  449 us (27%)
  matrix products  431 us (26%)
  other arithmetic  139 us (8%)
  blocking collectives  109 us (6%)
  loops' own time  48.6 us (3%)
    dynamic_update_slice x16, local copies, waits for them, and re-layouts, local(): lax.scan(forward_block, (zero_state, zero_total), jnp.arange(blocks, dtyp...  183 us
    reduce_scatter x1, waiting for transfers between devices, local(): lax.psum_scatter(jnp.dot(hidden_low, down_weight, preferred_element_type=...  76.8 us
    all_gather x1, waiting for transfers between devices, local(): group_second = lax.all_gather(second_low, 'mp', axis=0, tiled=True)  76.4 us
    psum x1, waiting for transfers between devices, local(): lax.psum((grad_qkv, grad_out, grad_gain_one, grad_shift_one, grad_gain_tw...  71.9 us
    all_gather x1, waiting for transfers between devices, local(): lax.all_gather(grad_context_own, 'mp', axis=0, tiled=True)  66.3 us
    all_gather x1, waiting for transfers between devices, local(): group_rows = lax.all_gather(normed_low, 'mp', axis=0, tiled=True)  62.3 us
    all_gather x1, waiting for transfers between devices, local(): group_cotangent = lax.all_gather(cotangent, 'mp', axis=0, tiled=True)  58 us
    reduce_scatter x1, waiting for transfers between devices, local(): lax.psum_scatter(jnp.einsum('tf,df->td', hidden_grad, up_weight, preferre...  55.1 us
  transfers between devices with their start and end apart: 8, of which 7 were waited for; matrix products, arithmetic and copies ran while one was open for 26% of the time, Pallas kernels for 0%

commit v1 on v0

--- a/solution.py
+++ b/solution.py
@@ -145,7 +145,14 @@
     inputs = tokens.astype(jnp.float32)
     normed_one, scaled_one, inv_one = normalize(inputs, norm1_gain, norm1_shift)
     normed_low = normed_one.astype(jnp.bfloat16)
-    group_rows = lax.all_gather(normed_low, "mp", axis=0, tiled=True)
+    ways = lax.axis_size("mp")
+    pieces = [normed_low]
+    for far in range(1, ways):
+        pieces.append(
+            lax.ppermute(pieces[far - 1], "mp", [(d, (d - 1) % ways) for d in range(ways)])
+        )
+    line = jnp.concatenate(pieces, axis=0)
+    group_rows = jnp.roll(line, lax.axis_index("mp") * normed_low.shape[0], axis=0)
 
     def features(start):
         rows_in = lax.dynamic_slice_in_dim(group_rows, start, BLK)

time: 1690 us -> 1700 us (level)
  local copies, waits for them, and re-layouts: 449 us -> 468 us
    all_gather x1 -> x0, waiting for transfers between devices: 62.3 us -> none  [local(): group_rows = lax.all_gather(normed_low, 'mp', axis=0, tiled=True)]
    ppermute x0 -> x3, waiting for transfers between devices: none -> 44 us  [local(): lax.ppermute(pieces[far - 1], 'mp', [(d, (d - 1) % ways) for d in range(w...]
    unnamed x126 -> x138, local copies, waits for them, and re-layouts: 33.2 us -> 44.7 us
  transfers between devices with their start and end apart: 8 -> 10, of which waited for: 7 -> 8; matrix products, arithmetic and copies ran while one was open for 26% -> 27% of each run, Pallas kernels for 0% -> 0%
where the time goes in v1:
time: 1700 us; the launch traced here: 1680 us
  local copies, waits for them, and re-layouts  468 us (28%)
  waiting for transfers between devices  462 us (27%)
  matrix products  431 us (25%)
  other arithmetic  139 us (8%)
  blocking collectives  105 us (6%)
  loops' own time  48.6 us (3%)
    dynamic_update_slice x16, local copies, waits for them, and re-layouts, local(): lax.scan(forward_block, (zero_state, zero_total), jnp.arange(blocks, dtyp...  183 us
    all_gather x1, waiting for transfers between devices, local(): group_second = lax.all_gather(second_low, 'mp', axis=0, tiled=True)  78.9 us
    reduce_scatter x1, waiting for transfers between devices, local(): lax.psum_scatter(jnp.dot(hidden_low, down_weight, preferred_element_type=...  76.8 us
    psum x1, waiting for transfers between devices, local(): lax.psum((grad_qkv, grad_out, grad_gain_one, grad_shift_one, grad_gain_tw...  71.6 us
    all_gather x1, waiting for transfers between devices, local(): lax.all_gather(grad_context_own, 'mp', axis=0, tiled=True)  66.3 us
    reduce_scatter x1, waiting for transfers between devices, local(): lax.psum_scatter(jnp.einsum('tf,df->td', hidden_grad, up_weight, preferre...  65.3 us
    all_gather x1, waiting for transfers between devices, local(): group_cotangent = lax.all_gather(cotangent, 'mp', axis=0, tiled=True)  58.1 us
    dot_general x8, matrix products, forward_block(): jnp.einsum('ihd,jhd->hij', query_low, key_low, preferred_element_type=jnp...  46.3 us
  transfers between devices with their start and end apart: 10, of which 8 were waited for; matrix products, arithmetic and copies ran while one was open for 27% of the time, Pallas kernels for 0%

profile of v1, /device:TPU:0, one launch (start us, length us, event | category | flops | bytes accessed | tf_op | source)
XLA Modules:
  0.0 1684.2 jit_solution(15356356037390488397)
XLA Ops:
  15.9 22.4 %collective-permute-done = bf16[1024,512]{0,1:T(8,128)(2,1)S(1)} collective-permute-done((bf16[1024,512]{0,1:T(8,128)(2,1)S(1)}, bf16[1024,512]{0,1:T(8,128)(2,1)S(1)}, u32[]{:S(2)}, u32[]{:S(2)}) %collective-permute-start) | collective-permute-done | bytes 1048608 | tf_op jit(solution)/shard_map/ppermute | solution.py:152
  43.6 21.6 %collective-permute-done.1 = bf16[1024,512]{0,1:T(8,128)(2,1)} collective-permute-done((bf16[1024,512]{0,1:T(8,128)(2,1)S(1)}, bf16[1024,512]{0,1:T(8,128)(2,1)}, u32[]{:S(2)}, u32[]{:S(2)}) %collective-permute-start.1) | collective-permute-done | bytes 1048608 | tf_op jit(solution)/shard_map/ppermute | solution.py:152
  75.5 12.0 all-reduce
  112.7 483.1 %while.75 = (s32[]{:T(128)}, f32[8,64,64]{2,1,0:T(8,128)S(1)}, f32[8,64]{1,0:T(8,128)S(1)}, f32[8,512,8,64]{1,0,3,2:T(8,128)}, f32[8,512,8]{1,2,0:T(8,128)}, /*i...) while((s32[]{:T(128)}, f32[8,64,64]{2,1,0:T(8,128)S(1)}, ...), condition=%wide.region_8.9_spmd.clone, body=%wide.region_5.8_spmd.clone.sunk | while | flops 1599254528 | bytes 64349520 | solution.py:203
  143.8 21.8 %dynamic_update_slice.51 = f32[8,512,8,64]{1,0,3,2:T(8,128)} dynamic-update-slice(f32[8,512,8,64]{1,0,3,2:T(8,128)} %get-tuple-element.1295, f32[1,512,8,64]{1,0,3,2:T(1,128)S(1)} %copy.224, s32[]{:T(128)} %get-tuple-element.1292, s32[]{:T(128)} %constant.271.clone.1..sunk.2, s32[]{:T(128)} %constant.271.clone.1..sunk.2, s32[]{:T(128)} %constant.271.clone.1..sunk.2) | dynamic-update-slice | bytes 2097156 | tf_op jit(solution)/shard_map/while/body/jit(dynamic_update_index_in_dim)/dynamic_update_slice | solution.py:203
  204.2 21.8 %dynamic_update_slice.51 = f32[8,512,8,64]{1,0,3,2:T(8,128)} dynamic-update-slice(f32[8,512,8,64]{1,0,3,2:T(8,128)} %get-tuple-element.1295, f32[1,512,8,64]{1,0,3,2:T(1,128)S(1)} %copy.224, s32[]{:T(128)} %get-tuple-element.1292, s32[]{:T(128)} %constant.271.clone.1..sunk.2, s32[]{:T(128)} %constant.271.clone.1..sunk.2, s32[]{:T(128)} %constant.271.clone.1..sunk.2) | dynamic-update-slice | bytes 2097156 | tf_op jit(solution)/shard_map/while/body/jit(dynamic_update_index_in_dim)/dynamic_update_slice | solution.py:203
  264.6 21.8 %dynamic_update_slice.51 = f32[8,512,8,64]{1,0,3,2:T(8,128)} dynamic-update-slice(f32[8,512,8,64]{1,0,3,2:T(8,128)} %get-tuple-element.1295, f32[1,512,8,64]{1,0,3,2:T(1,128)S(1)} %copy.224, s32[]{:T(128)} %get-tuple-element.1292, s32[]{:T(128)} %constant.271.clone.1..sunk.2, s32[]{:T(128)} %constant.271.clone.1..sunk.2, s32[]{:T(128)} %constant.271.clone.1..sunk.2) | dynamic-update-slice | bytes 2097156 | tf_op jit(solution)/shard_map/while/body/jit(dynamic_update_index_in_dim)/dynamic_update_slice | solution.py:203
  325.0 21.8 %dynamic_update_slice.51 = f32[8,512,8,64]{1,0,3,2:T(8,128)} dynamic-update-slice(f32[8,512,8,64]{1,0,3,2:T(8,128)} %get-tuple-element.1295, f32[1,512,8,64]{1,0,3,2:T(1,128)S(1)} %copy.224, s32[]{:T(128)} %get-tuple-element.1292, s32[]{:T(128)} %constant.271.clone.1..sunk.2, s32[]{:T(128)} %constant.271.clone.1..sunk.2, s32[]{:T(128)} %constant.271.clone.1..sunk.2) | dynamic-update-slice | bytes 2097156 | tf_op jit(solution)/shard_map/while/body/jit(dynamic_update_index_in_dim)/dynamic_update_slice | solution.py:203
  385.4 21.8 %dynamic_update_slice.51 = f32[8,512,8,64]{1,0,3,2:T(8,128)} dynamic-update-slice(f32[8,512,8,64]{1,0,3,2:T(8,128)} %get-tuple-element.1295, f32[1,512,8,64]{1,0,3,2:T(1,128)S(1)} %copy.224, s32[]{:T(128)} %get-tuple-element.1292, s32[]{:T(128)} %constant.271.clone.1..sunk.2, s32[]{:T(128)} %constant.271.clone.1..sunk.2, s32[]{:T(128)} %constant.271.clone.1..sunk.2) | dynamic-update-slice | bytes 2097156 | tf_op jit(solution)/shard_map/while/body/jit(dynamic_update_index_in_dim)/dynamic_update_slice | solution.py:203
  445.7 21.8 %dynamic_update_slice.51 = f32[8,512,8,64]{1,0,3,2:T(8,128)} dynamic-update-slice(f32[8,512,8,64]{1,0,3,2:T(8,128)} %get-tuple-element.1295, f32[1,512,8,64]{1,0,3,2:T(1,128)S(1)} %copy.224, s32[]{:T(128)} %get-tuple-element.1292, s32[]{:T(128)} %constant.271.clone.1..sunk.2, s32[]{:T(128)} %constant.271.clone.1..sunk.2, s32[]{:T(128)} %constant.271.clone.1..sunk.2) | dynamic-update-slice | bytes 2097156 | tf_op jit(solution)/shard_map/while/body/jit(dynamic_update_index_in_dim)/dynamic_update_slice | solution.py:203
  506.1 21.8 %dynamic_update_slice.51 = f32[8,512,8,64]{1,0,3,2:T(8,128)} dynamic-update-slice(f32[8,512,8,64]{1,0,3,2:T(8,128)} %get-tuple-element.1295, f32[1,512,8,64]{1,0,3,2:T(1,128)S(1)} %copy.224, s32[]{:T(128)} %get-tuple-element.1292, s32[]{:T(128)} %constant.271.clone.1..sunk.2, s32[]{:T(128)} %constant.271.clone.1..sunk.2, s32[]{:T(128)} %constant.271.clone.1..sunk.2) | dynamic-update-slice | bytes 2097156 | tf_op jit(solution)/shard_map/while/body/jit(dynamic_update_index_in_dim)/dynamic_update_slice | solution.py:203
  566.5 21.8 %dynamic_update_slice.51 = f32[8,512,8,64]{1,0,3,2:T(8,128)} dynamic-update-slice(f32[8,512,8,64]{1,0,3,2:T(8,128)} %get-tuple-element.1295, f32[1,512,8,64]{1,0,3,2:T(1,128)S(1)} %copy.224, s32[]{:T(128)} %get-tuple-element.1292, s32[]{:T(128)} %constant.271.clone.1..sunk.2, s32[]{:T(128)} %constant.271.clone.1..sunk.2, s32[]{:T(128)} %constant.271.clone.1..sunk.2) | dynamic-update-slice | bytes 2097156 | tf_op jit(solution)/shard_map/while/body/jit(dynamic_update_index_in_dim)/dynamic_update_slice | solution.py:203
  595.8 11.0 all-gather
  606.7 8.4 all-gather.1
  615.2 22.9 %while.76 = (s32[]{:T(128)}, f32[8,64,64]{2,1,0:T(8,128)}, f32[8,64]{1,0:T(8,128)S(1)}, s32[]{:T(128)}, bf16[8,8,64,64]{3,2,1,0:T(8,128)(2,1)S(1)}, /*index=5*/b...) while((s32[]{:T(128)}, f32[8,64,64]{2,1,0:T(8,128)}, ...), condition=%wide.region_10.11_spmd.clone, body=%wide.region_9.10_spmd.clone.sunk | while | flops 166405 | bytes 332957 | solution.py:34
  642.9 9.4 reshape.432
  671.3 78.9 %all-gather.8.cloned.1.call-done = bf16[4096,512]{0,1:T(8,128)(2,1)} async-done(((bf16[1024,512]{0,1:T(8,128)(2,1)}), bf16[4096,512]{0,1:T(8,128)(2,1)}) %all-gather.8.cloned.1.call-update) | async-done | bytes 4194320 | tf_op jit(solution)/shard_map/all_gather | solution.py:230
  750.2 22.8 %fusion.89 = (bf16[4096,512]{1,0:T(8,128)(2,1)}, f32[4096,512]{1,0:T(8,128)}) fusion(f32[512]{0:T(512)} %convert_element_type.335, bf16[4096,512]{0,1:T(8,128)(2,1)} %all-gather.8.cloned.1.call-done, bf16[512,512]{1,0:T(8,128)(2,1)S(1)} %copy-done), kind=kOutput, calls=%fused_computation.135 | convolution fusion | flops 2285895680 | bytes 17303552 | tf_op jit(solution)/shard_map/dot_general | solution.py:231
  773.0 58.1 %all-gather.10.cloned.1.call-done = bf16[4096,512]{1,0:T(8,128)(2,1)} async-done(((bf16[1024,512]{1,0:T(8,128)(2,1)}), bf16[4096,512]{1,0:T(8,128)(2,1)}) %all-gather.10.cloned.1.call-update) | async-done | bytes 4194320 | tf_op jit(solution)/shard_map/all_gather | solution.py:239
  831.0 8.9 convert_reduce_fusion.1
  856.4 65.3 %reduce-scatter.5.cloned.1.call-done = bf16[1024,512]{0,1:T(8,128)(2,1)} async-done(((bf16[4096,512]{0,1:T(8,128)(2,1)}), bf16[1024,512]{0,1:T(8,128)(2,1)}) %reduce-scatter.5.cloned.1.call-update) | async-done | bytes 1048592 | tf_op jit(solution)/shard_map/reduce_scatter | solution.py:249
  924.4 76.8 %reduce-scatter.3.cloned.1.call-done = bf16[1024,512]{0,1:T(8,128)(2,1)} async-done(((bf16[4096,512]{0,1:T(8,128)(2,1)}), bf16[1024,512]{0,1:T(8,128)(2,1)}) %reduce-scatter.3.cloned.1.call-update) | async-done | bytes 1048592 | tf_op jit(solution)/shard_map/reduce_scatter | solution.py:233
  1024.1 66.3 %all-gather.12.cloned.1.call-done = bf16[4096,512]{1,0:T(8,128)(2,1)} async-done(((bf16[1024,512]{1,0:T(8,128)(2,1)}), bf16[4096,512]{1,0:T(8,128)(2,1)}) %all-gather.12.cloned.1.call-update) | async-done | bytes 4194320 | tf_op jit(solution)/shard_map/all_gather | solution.py:271
  1090.4 7.0 copy.158
  1097.4 7.8 multiply_reduce_fusion.1
  1111.0 8.9 all-gather.3
  1124.0 13.2 all-gather.2
  1137.2 9.7 while.73
  1152.6 371.5 %while.74 = (s32[]{:T(128)}, f32[8,64,64]{2,1,0:T(8,128)S(1)}, f32[8,64]{1,0:T(8,128)S(1)}, bf16[8,512,1536]{2,1,0:T(8,128)(2,1)}, s32[8]{0:T(128)S(1)}, /*index...) while((s32[]{:T(128)}, f32[8,64,64]{2,1,0:T(8,128)S(1)}, ...), condition=%wide.region_21.22_spmd, body=%wide.region_20.21_spmd.sunk | while | flops 2815500288 | bytes 89005016 | solution.py:359
  1530.4 12.9 psum.77
  1559.6 39.1 %all-reduce.1 = (f32[512]{0:T(512)}, f32[512]{0:T(512)}, f32[512]{0:T(512)}, f32[512]{0:T(512)}, f32[512]{0:T(512)}) all-reduce(f32[512]{0:T(512)S(1)} %get-tuple-element.848, f32[512]{0:T(512)S(1)} %get-tuple-element.979, f32[512]{0:T(512)S(1)} %copy-done.51, f32[512]{0:T(512)S(1)} %copy-done.52, ...), channel_id=1, replica_groups=mesh['dp'=8,'mp'=4] {'dp','mp'}, use_global_device_ids=true, to_apply=%region_27.28 | all-reduce | flops 2560 | bytes 20480 | tf_op jit(solution)/shard_map/psum | solution.py:374
  1598.7 71.6 %all-reduce.7.cloned.1.call-done = (f32[512,1536]{1,0:T(8,128)}, f32[512,512]{1,0:T(8,128)}) async-done(((f32[512,1536]{1,0:T(8,128)}, f32[512,512]{1,0:T(8,128)}), (f32[512,1536]{1,0:T(8,128)}, f32[512,512]{1,0:T(8,128)})) %all-reduce.7.cloned.1.call-update) | async-done | bytes 4194320 | tf_op jit(solution)/shard_map/psum | solution.py:374
  (774 shorter events, 822.9 us)
Async XLA Ops:
  7.2 743.0 %copy-start = (bf16[512,512]{1,0:T(8,128)(2,1)S(1)}, bf16[512,512]{1,0:T(8,128)(2,1)}, u32[]{:S(2)}) copy-start(bf16[512,512]{1,0:T(8,128)(2,1)} %param.28) | copy-start | bytes 1572868
  7.2 66.3 %copy-start.62 = (u32[32]{0:T(128)S(1)}, u32[32]{0:T(128)}, u32[]{:S(2)}) copy-start(u32[32]{0:T(128)} %constant.319) | copy-start | bytes 388
  7.2 62.3 %copy-start.57 = (s32[17]{0:T(128)S(1)}, s32[17]{0:T(128)}, u32[]{:S(2)}) copy-start(s32[17]{0:T(128)} %param.32) | copy-start | bytes 208
  7.2 743.0 %all-gather.8.cloned.1.call-start = ((), (), s32[]{:S(2)}) async-start(), calls=%async_computation.2 | async-start | bytes 5242880 | tf_op jit(solution)/shard_map/all_gather | solution.py:230
  8.8 83.5 %copy-start.7 = (bf16[1024,512]{0,1:T(8,128)(2,1)}, bf16[1024,512]{0,1:T(8,128)(2,1)S(1)}, u32[]{:S(2)}) copy-start(bf16[1024,512]{0,1:T(8,128)(2,1)S(1)} %copy.149) | copy-start | bytes 3145732
  9.0 56.1 %copy-start.37 = (f32[1024]{0:T(1024)}, f32[1024]{0:T(1024)S(1)}, u32[]{:S(2)}) copy-start(f32[1024]{0:T(1024)S(1)} %broadcast_multiply_fusion.5) | copy-start | bytes 12292
  9.4 60.1 %copy-start.41 = (f32[1024]{0:T(1024)}, f32[1024]{0:T(1024)S(1)}, u32[]{:S(2)}) copy-start(f32[1024]{0:T(1024)S(1)} %add_rsqrt_fusion.1) | copy-start | bytes 12292
  10.8 84.9 %copy-start.21 = (bf16[1024,512]{0,1:T(8,128)(2,1)}, bf16[1024,512]{0,1:T(8,128)(2,1)S(1)}, u32[]{:S(2)}) copy-start(bf16[1024,512]{0,1:T(8,128)(2,1)S(1)} %get-tuple-element.955) | copy-start | bytes 3145732
  10.8 27.5 %collective-permute-start = (bf16[1024,512]{0,1:T(8,128)(2,1)S(1)}, bf16[1024,512]{0,1:T(8,128)(2,1)S(1)}, u32[]{:S(2)}, u32[]{:S(2)}) collective-permute-start(bf16[1024,512]{0,1:T(8,128)(2,1)S(1)} %get-tuple-element.955), channel_id=1, source_target_pairs={{0,3},{1,0},{2,1},{3,2},{4,7},{5,4},{6,5},{7,6},{8,11},{9,8},{10,9... | collective-permute-start | bytes 3145736 | tf_op jit(solution)/shard_map/ppermute | solution.py:152
  39.3 25.8 %collective-permute-start.1 = (bf16[1024,512]{0,1:T(8,128)(2,1)S(1)}, bf16[1024,512]{0,1:T(8,128)(2,1)}, u32[]{:S(2)}, u32[]{:S(2)}) collective-permute-start(bf16[1024,512]{0,1:T(8,128)(2,1)S(1)} %collective-permute-done), channel_id=1, source_target_pairs={{0,3},{1,0},{2,1},{3,2},{4,7},{5,4},{6,5},{7,6},{8,11},{9,8},{10,9... | collective-permute-start | bytes 3145736 | tf_op jit(solution)/shard_map/ppermute | solution.py:152
  65.1 27.1 %collective-permute-start.2 = (bf16[1024,512]{0,1:T(8,128)(2,1)}, bf16[1024,512]{0,1:T(8,128)(2,1)}, u32[]{:S(2)}, u32[]{:S(2)}) collective-permute-start(bf16[1024,512]{0,1:T(8,128)(2,1)} %collective-permute-done.1), channel_id=1, source_target_pairs={{0,3},{1,0},{2,1},{3,2},{4,7},{5,4},{6,5},{7,6},{8,11},{9,8},{10,9... | collective-permute-start | bytes 3145736 | tf_op jit(solution)/shard_map/ppermute | solution.py:152
  72.9 22.8 %copy-start.31 = (f32[4096]{0:T(1024)}, f32[4096]{0:T(1024)S(1)}, u32[]{:S(2)}) copy-start(f32[4096]{0:T(1024)S(1)} %get-tuple-element.953) | copy-start | bytes 49156
  87.6 8.2 copy-start.23
  595.7 11.0 copy-start.48
  638.1 14.3 copy-start.29
  642.9 13.5 copy-start.32
  642.9 13.5 copy-start.34
  656.5 7.0 copy-start.8
  656.6 7.0 copy-start.25
  669.3 161.8 %all-gather.10.cloned.1.call-start = ((), (), s32[]{:S(2)}) async-start(), calls=%async_computation.4 | async-start | bytes 5242880 | tf_op jit(solution)/shard_map/all_gather | solution.py:239
  670.0 251.7 %reduce-scatter.5.cloned.1.call-start = ((), (), s32[]{:S(2)}) async-start(), calls=%async_computation.5 | async-start | bytes 5242880 | tf_op jit(solution)/shard_map/reduce_scatter | solution.py:249
  846.3 154.9 %reduce-scatter.3.cloned.1.call-start = ((), (), s32[]{:S(2)}) async-start(), calls=%async_computation.3 | async-start | bytes 5242880 | tf_op jit(solution)/shard_map/reduce_scatter | solution.py:233
  853.9 67.9 %copy-start.36 = (f32[1024]{0:T(1024)S(1)}, f32[1024]{0:T(1024)}, u32[]{:S(2)}) copy-start(f32[1024]{0:T(1024)} %copy-done.35) | copy-start | bytes 12292
  853.9 67.9 %copy-start.40 = (f32[1024]{0:T(1024)S(1)}, f32[1024]{0:T(1024)}, u32[]{:S(2)}) copy-start(f32[1024]{0:T(1024)} %copy-done.39) | copy-start | bytes 12292
  853.9 67.9 %copy-start.47 = (f32[512]{0:T(512)S(1)}, f32[512]{0:T(512)}, u32[]{:S(2)}) copy-start(f32[512]{0:T(512)} %param.26) | copy-start | bytes 6148
  853.9 147.3 %copy-start.55 = (f32[512]{0:T(512)S(1)}, f32[512]{0:T(512)}, u32[]{:S(2)}) copy-start(f32[512]{0:T(512)} %param.31) | copy-start | bytes 6148
  853.9 236.5 %all-gather.12.cloned.1.call-start = ((), (), s32[]{:S(2)}) async-start(), calls=%async_computation.6 | async-start | bytes 5242880 | tf_op jit(solution)/shard_map/all_gather | solution.py:271
  1009.0 589.7 %all-reduce.9.cloned.1.call-start = ((), (), s32[]{:S(2)}) async-start(), calls=%async_computation.8 | async-start | bytes 4194304 | tf_op jit(solution)/shard_map/psum | solution.py:257
  1020.7 649.5 %all-reduce.7.cloned.1.call-start = ((), (), s32[]{:S(2)}) async-start(), calls=%async_computation.7 | async-start | bytes 8388608 | tf_op jit(solution)/shard_map/psum | solution.py:374
  1097.4 22.5 %copy-start.5 = (f32[4096,512]{0,1:T(8,128)S(1)}, f32[4096,512]{0,1:T(8,128)}, u32[]{:S(2)}) copy-start(f32[4096,512]{0,1:T(8,128)} %copy.158) | copy-start | bytes 25165828
  1122.8 14.5 copy-start.61
  1529.7 13.6 copy-start.20
  (70 other events, 228.6 us)
Sparse Core Ops, SparseCore 0:
  669.4 80.7 all-gather.7
  751.8 79.2 all-gather.9
  846.4 75.2 reduce-scatter.4
  923.9 77.2 reduce-scatter.2
  1009.1 81.2 all-gather.11
  1093.5 61.3 all-reduce.8
  1529.9 140.3 all-reduce.6
